TPU v7x, 256 devices: a whole 4x4x8 slice. The times are simulated.
256 devices in a mesh: sub: 32 (over x, z), vec: 8 (over y, core).
Axes of the slice: x: 4, y: 4, z: 8, core: 2. Of those that a mesh axis runs over, the one named last changes fastest.
Arguments:
- coefficients: bfloat16 [1024, 20480], P('sub', 'vec'), may hold values from -6 to 6
- row_counts: int32 [32], replicated, may hold values from 1 to 1024, 16384 in all
- ancestors: int32 [32, 3], replicated, may hold values from 0 to 27, as said below
- interior_modes: bfloat16 [131072, 1024], P('sub'), may hold values from -0.25 to 0.25
- separator_modes: bfloat16 [8192, 128], replicated, may hold values from -0.5 to 0.5
- coupling: bfloat16 [131072, 768], P('sub'), may hold values from -0.3125 to 0.3125
- pattern: int32 [32, 16, 3], P('sub'), may hold values 0 or 1
Outputs:
- interior_field: bfloat16 [131072, 1024], P('sub', 'vec')
- separator_field: bfloat16 [8192, 1024], P('sub', 'vec')
Inputs may be any that keep to these rules, and one draw needn't show every extreme that they name: `ancestors`: the separators form binary trees: substructures pair under level-1 separators, pairs of those under level-2 separators, and so on, so that a level-l separator lies over 2**l substructures; no separator appears at two levels. `row_counts`: the counts sum to 512 * 32.
All inputs are finite; a program needn't handle non-finite values. No bound on the sum of `pattern` on one device may be relied on, other than what follows from the above.
Results may differ from a plain program's by a relative error of at most 0.0038.
Values may be sent and summed in bfloat16 or wider, within the bound.
A program may use at most 128 MiB of HBM per device.

v0:
```python
import jax
import jax.numpy as jnp
from jax import lax
from jax.sharding import PartitionSpec as P

BW = 256
SEPM = 128
LEVELS = 3


def window_rows(full_rows, row_counts, interior_total, cap_rows):
    slice_cols = full_rows.shape[0]
    block_total = interior_total // cap_rows + 1
    padded = jnp.concatenate(
        [full_rows[:, :interior_total], jnp.zeros((slice_cols, cap_rows), full_rows.dtype)], axis=1
    )
    blocks = padded.reshape(slice_cols, block_total, cap_rows)
    offsets = jnp.cumsum(row_counts) - row_counts
    first_block = offsets // cap_rows
    remainder = offsets - first_block * cap_rows
    labels = jnp.arange(block_total, dtype=jnp.int32)
    pick_first = (first_block[:, None] == labels[None, :]).astype(blocks.dtype)
    pick_second = (first_block[:, None] + 1 == labels[None, :]).astype(blocks.dtype)
    lower = jnp.einsum("ob,cbj->ocj", pick_first, blocks, preferred_element_type=jnp.float32)
    upper = jnp.einsum("ob,cbj->ocj", pick_second, blocks, preferred_element_type=jnp.float32)
    window = jnp.concatenate([lower, upper], axis=2).astype(blocks.dtype)
    for bit in range(cap_rows.bit_length() - 1):
        amount = 1 << bit
        moved = jnp.concatenate(
            [window[:, :, amount:], jnp.zeros(window.shape[:2] + (amount,), window.dtype)], axis=2
        )
        flag = remainder >> bit & 1 == 1
        window = jnp.where(flag[:, None, None], moved, window)
    window = window[:, :, :cap_rows]
    positions = jnp.arange(cap_rows, dtype=jnp.int32)
    live = positions[None, :] < row_counts[:, None]
    window = jnp.where(live[:, None, :], window, jnp.zeros((), window.dtype))
    return jnp.transpose(window, (1, 0, 2))


def body(coefficients, row_counts, ancestors, interior_modes, separator_modes, coupling, pattern):
    sub_count = lax.axis_size("sub")
    vec_count = lax.axis_size("vec")
    my_index = lax.axis_index("sub")
    slice_cols = coefficients.shape[0] // vec_count
    rows_vec = coefficients.shape[1]
    regrouped = coefficients.reshape(vec_count, slice_cols, rows_vec)
    full_rows = lax.all_to_all(regrouped, "vec", split_axis=0, concat_axis=2, tiled=True)
    full_rows = full_rows.reshape(slice_cols, vec_count * rows_vec)
    total_rows = full_rows.shape[1]
    interior_total = total_rows - sub_count * SEPM
    cap_rows = interior_modes.shape[1]
    interior_part = window_rows(full_rows, row_counts, interior_total, cap_rows)
    sep_part = full_rows[:, interior_total:].reshape(slice_cols, sub_count, SEPM)
    parts = [interior_part, sep_part]
    picked = jnp.concatenate(parts, axis=2)
    slot_width = picked.shape[2]
    received = lax.all_to_all(picked, "sub", split_axis=1, concat_axis=0, tiled=True)
    group_cols = sub_count * slice_cols
    received = received.reshape(group_cols, slot_width)
    interior_coef = received[:, :cap_rows]
    own_coef = received[:, cap_rows : cap_rows + SEPM]
    modes_by_sep = separator_modes.reshape(sub_count, BW, SEPM)
    own_modes = lax.dynamic_index_in_dim(modes_by_sep, my_index, 0, keepdims=False)
    contract = (((1,), (1,)), ((), ()))
    own_field = lax.dot_general(
        own_modes, own_coef, contract, preferred_element_type=jnp.float32
    ).astype(jnp.bfloat16)
    interior_sum = lax.dot_general(
        interior_modes, interior_coef, contract, preferred_element_type=jnp.float32
    )
    my_ancestors = lax.dynamic_index_in_dim(ancestors, my_index, 0, keepdims=False)
    piece = lax.all_gather(own_field[None], "sub", axis=0, tiled=True)
    labels = jnp.arange(piece.shape[0], dtype=jnp.int32)
    select = (my_ancestors[:, None] == labels[None, :]).astype(piece.dtype)
    ancestor_blocks = jnp.einsum(
        "lc,cbk->lbk", select, piece, preferred_element_type=jnp.float32
    ).astype(jnp.bfloat16)
    block_count = coupling.shape[0] // BW
    gates = pattern[0].astype(coupling.dtype)
    masked = (coupling.reshape(block_count, BW, LEVELS, BW) * gates[:, None, :, None]).reshape(
        coupling.shape
    )
    interior_sum = interior_sum + jnp.dot(
        masked, ancestor_blocks.reshape(LEVELS * BW, group_cols), preferred_element_type=jnp.float32
    )
    return (interior_sum.astype(jnp.bfloat16), own_field)


def solution(mesh):
    placed = (P("sub", "vec"), P(), P(), P("sub", None), P(), P("sub", None), P("sub", None, None))
    return jax.shard_map(
        body,
        mesh=mesh,
        in_specs=placed,
        out_specs=(P("sub", "vec"), P("sub", "vec")),
        check_vma=False,
    )
```

profile of v0, /device:TPU:8, one launch (start us, length us, event | category | flops | bytes accessed | tf_op | source)
XLA Modules:
  0.0 143.3 jit_solution(3298135842300496320)
XLA Ops:
  7.2 0.0 copy-start
  7.2 1.8 %reshape.96 = bf16[8,4,2560]{2,1,0:T(4,128)(2,1)} reshape(bf16[32,2560]{1,0:T(8,128)(2,1)} %param.7) | data formatting | bytes 327680 | tf_op jit(solution)/shard_map/reshape | solution.py:47
  9.0 5.4 %all-to-all-start = ((bf16[8,4,2560]{2,1,0:T(4,128)(2,1)}), bf16[8,4,2560]{2,1,0:T(4,128)(2,1)S(1)}, u32[]{:S(2)}, u32[]{:S(2)}) async-start(bf16[8,4,2560]{2,1,0:T(4,128)(2,1)} %reshape.96), calls=%async_computation | async-start | bytes 327680 | tf_op jit(solution)/shard_map/all_to_all | solution.py:48
  14.4 0.7 iota_compare_fusion
  15.1 0.7 copy.21
  15.9 0.1 reduce-window.9
  15.9 0.1 reduce
  16.1 0.7 and_compare_fusion.9
  16.8 2.7 %all-to-all-done = bf16[8,4,2560]{2,1,0:T(4,128)(2,1)S(1)} async-done(((bf16[8,4,2560]{2,1,0:T(4,128)(2,1)}), bf16[8,4,2560]{2,1,0:T(4,128)(2,1)S(1)}, u32[]{:S(2)}, u32[]{:S(2)}) %all-to-all-start) | async-done | bytes 163872 | tf_op jit(solution)/shard_map/all_to_all | solution.py:48
  19.4 0.8 slice_select_fusion.1
  20.3 0.1 reshape.98
  20.4 0.3 convolution_convert_fusion.1
  20.7 0.3 convolution_convert_fusion
  20.9 0.2 fusion.9
  21.2 0.2 fusion.10
  21.4 0.2 slice.64
  21.6 0.2 pad_select_fusion.7
  21.8 0.2 slice.65
  22.0 0.2 pad_select_fusion.6
  22.2 0.2 slice.66
  22.4 0.2 pad_select_fusion.5
  22.7 0.2 slice.67
  22.9 0.2 pad_select_fusion.4
  23.1 0.2 slice.68
  23.3 0.2 pad_select_fusion.3
  23.5 0.0 copy-start.1
  23.5 0.2 slice.69
  23.7 0.2 pad_select_fusion.2
  24.0 0.2 pad_select_fusion.1
  24.2 0.2 pad_select_fusion
  24.5 0.2 fusion.13
  24.7 0.9 copy.22
  25.5 10.7 %all-to-all-start.1 = ((bf16[4,32,1152]{2,0,1:T(4,128)(2,1)}), bf16[4,32,1152]{2,0,1:T(4,128)(2,1)S(1)}, u32[]{:S(2)}, u32[]{:S(2)}) async-start(bf16[4,32,1152]{2,0,1:T(4,128)(2,1)} %copy.22), calls=%async_computation.1 | async-start | bytes 589824 | tf_op jit(solution)/shard_map/all_to_all | solution.py:58
  36.3 0.2 all-gather.3.cloned.1.call-start
  36.5 12.5 %all-to-all-done.1 = bf16[4,32,1152]{2,0,1:T(4,128)(2,1)S(1)} async-done(((bf16[4,32,1152]{2,0,1:T(4,128)(2,1)}), bf16[4,32,1152]{2,0,1:T(4,128)(2,1)S(1)}, u32[]{:S(2)}, u32[]{:S(2)}) %all-to-all-start.1) | async-done | bytes 294944 | tf_op jit(solution)/shard_map/all_to_all | solution.py:58
  49.0 0.1 reshape.100
  49.1 0.8 convolution_convert_fusion.2
  49.9 0.0 all-gather.3.cloned.1.call-update
  49.9 0.2 dynamic-slice_reduce_fusion
  50.1 0.5 mul.16
  50.6 6.8 %copy.31 = bf16[96,8,16,256]{3,1,2,0:T(8,128)(2,1)} copy(bf16[96,8,16,256]{3,2,1,0:T(8,128)(2,1)S(1)} %bitcast.53) | data formatting | bytes 12582912
  57.5 8.8 %copy.23 = bf16[4096,768]{0,1:T(8,128)(2,1)} copy(bf16[4096,768]{1,0:T(8,128)(2,1)} %param.12) | data formatting | bytes 12582912 | tf_op args[5]
  66.2 56.9 %all-gather.3.cloned.1.call-done = bf16[8192,128]{1,0:T(8,128)(2,1)} async-done(((bf16[256,128]{1,0:T(8,128)(2,1)}), bf16[8192,128]{1,0:T(8,128)(2,1)}) %all-gather.3.cloned.1.call-update) | async-done | bytes 2097168 | tf_op jit(solution)/shard_map/all_gather | solution.py:73
  123.1 3.0 %fusion.6 = bf16[3,256,128]{2,0,1:T(4,128)(2,1)S(1)} fusion(bf16[32,256,128]{2,1,0:T(8,128)(2,1)} %bitcast.56, s32[3]{0:T(128)S(1)} %dynamic-slice_reduce_fusion), kind=kOutput, calls=%fused_computation.9 | convolution fusion | flops 6389856 | bytes 2293772 | tf_op jit(solution)/shard_map/lc,cbk->lbk/dot_general | solution.py:76
  126.1 0.0 slice-start.1
  126.1 6.1 %fusion = f32[4096,128]{0,1:T(8,128)S(1)} fusion(bf16[768,128]{1,0:T(8,128)(2,1)S(1)} %bitcast.58, bf16[4096,768]{0,1:T(8,128)(2,1)} %copy.23, bf16[4096,768]{0,1:T(8,128)(2,1)} %bitcast.52), kind=kOutput, calls=%fused_computation | convolution fusion | flops 808452096 | bytes 14876672 | tf_op jit(solution)/shard_map/dot_general | solution.py:84
  132.2 2.9 %fusion.3 = bf16[4096,128]{0,1:T(8,128)(2,1)S(1)} fusion(f32[4096,128]{0,1:T(8,128)S(1)} %fusion, bf16[4096,1024]{1,0:T(8,128)(2,1)S(1)} %bitcast.55, bf16[128,1152]{1,0:T(8,128)(2,1)S(1)} %reshape.100), kind=kOutput, calls=%fused_computation.4 | convolution fusion | flops 1074790400 | bytes 11796480 | tf_op jit(solution)/shard_map/dot_general | solution.py:69
  135.1 1.3 copy.27
  (19 shorter events, 0.2 us)
Async XLA Ops:
  7.2 41.9 %copy-start = (bf16[8192,128]{1,0:T(8,128)(2,1)S(1)}, bf16[8192,128]{1,0:T(8,128)(2,1)}, u32[]{:S(2)}) copy-start(bf16[8192,128]{1,0:T(8,128)(2,1)} %param.11) | copy-start | bytes 6291460
  9.0 10.5 %all-to-all-start = ((bf16[8,4,2560]{2,1,0:T(4,128)(2,1)}), bf16[8,4,2560]{2,1,0:T(4,128)(2,1)S(1)}, u32[]{:S(2)}, u32[]{:S(2)}) async-start(bf16[8,4,2560]{2,1,0:T(4,128)(2,1)} %reshape.96), calls=%async_computation | async-start | bytes 327680 | tf_op jit(solution)/shard_map/all_to_all | solution.py:48
  23.5 26.4 %copy-start.1 = (s32[32,3]{0,1:T(4,128)S(1)}, s32[32,3]{0,1:T(4,128)}, u32[]{:S(2)}) copy-start(s32[32,3]{0,1:T(4,128)} %param.9) | copy-start | bytes 1156
  23.5 26.6 %copy-start.2 = (s32[1,16,3]{1,0,2:T(1,128)S(1)}, s32[1,16,3]{1,0,2:T(1,128)}, u32[]{:S(2)}) copy-start(s32[1,16,3]{1,0,2:T(1,128)} %param.13) | copy-start | bytes 580
  25.5 23.5 %all-to-all-start.1 = ((bf16[4,32,1152]{2,0,1:T(4,128)(2,1)}), bf16[4,32,1152]{2,0,1:T(4,128)(2,1)S(1)}, u32[]{:S(2)}, u32[]{:S(2)}) async-start(bf16[4,32,1152]{2,0,1:T(4,128)(2,1)} %copy.22), calls=%async_computation.1 | async-start | bytes 589824 | tf_op jit(solution)/shard_map/all_to_all | solution.py:58
  36.3 86.8 %all-gather.3.cloned.1.call-start = ((), (), s32[]{:S(2)}) async-start(), calls=%async_computation.2 | async-start | bytes 2162688 | tf_op jit(solution)/shard_map/all_gather | solution.py:73
  123.1 9.1 %slice-start = ((s8[8388608]{0:T(1024)(128)(4,1)}), s8[4194304]{0:T(1024)(128)(4,1)S(1)}, s32[]{:S(2)}) async-start(s8[8388608]{0:T(1024)(128)(4,1)} %bitcast.54), calls=%async_computation.3 | async-start | bytes 8388608
  126.1 6.1 %slice-start.1 = ((s8[8388608]{0:T(1024)(128)(4,1)}), s8[4194304]{0:T(1024)(128)(4,1)S(1)}, s32[]{:S(2)}) async-start(s8[8388608]{0:T(1024)(128)(4,1)} %bitcast.54), calls=%async_computation.4 | async-start | bytes 8388608
Sparse Core Ops, SparseCore 0:
  50.0 72.9 all-gather.2
where the time goes:
time: 144 us; the launch traced here: 143 us
  waiting for transfers between devices  72 us (50%)
  local copies, waits for them, and re-layouts  22.5 us (16%)
  starting transfers between devices  16.4 us (11%)
  between operations  14.4 us (10%)
  matrix products  13.3 us (9%)
  other arithmetic  4.63 us (3%)
    all_gather x1, waiting for transfers between devices, body(): piece = lax.all_gather(own_field[None], 'sub', axis=0, tiled=True)  56.9 us
    unnamed x16, local copies, waits for them, and re-layouts  17 us
    all_to_all x1, waiting for transfers between devices, body(): lax.all_to_all(picked, 'sub', split_axis=1, concat_axis=0, tiled=True)  12.5 us
    all_to_all x1, starting transfers between devices, body(): lax.all_to_all(picked, 'sub', split_axis=1, concat_axis=0, tiled=True)  10.7 us
    dot_general x1, matrix products, body(): jnp.dot(masked, ancestor_blocks.reshape(LEVELS * BW, group_cols), preferr...  6.06 us
    all_to_all x1, starting transfers between devices, body(): lax.all_to_all(regrouped, 'vec', split_axis=0, concat_axis=2, tiled=True)  5.45 us
    dot_general x1, matrix products, body(): jnp.einsum('lc,cbk->lbk', select, piece, preferred_element_type=jnp.float32)  3 us
    dot_general x1, matrix products, body(): lax.dot_general(interior_modes, interior_coef, contract, preferred_elemen...  2.9 us
  transfers between devices with their start and end apart: 3, of which 3 were waited for; matrix products, arithmetic and copies ran while one was open for 13% of the time, Pallas kernels for 0%

commit v1 on v0

--- a/solution.py
+++ b/solution.py
@@ -70,7 +70,9 @@
         interior_modes, interior_coef, contract, preferred_element_type=jnp.float32
     )
     my_ancestors = lax.dynamic_index_in_dim(ancestors, my_index, 0, keepdims=False)
-    piece = lax.all_gather(own_field[None], "sub", axis=0, tiled=True)
+    piece = jnp.concatenate(
+        lax.all_to_all(jnp.stack([own_field[None]] * lax.axis_size("sub")), "sub", 0, 0), axis=0
+    )
     labels = jnp.arange(piece.shape[0], dtype=jnp.int32)
     select = (my_ancestors[:, None] == labels[None, :]).astype(piece.dtype)
     ancestor_blocks = jnp.einsum(

time: 144 us -> 113 us (0.78)
  waiting for transfers between devices: 72 us -> 47.9 us
  between operations: 14.4 us -> 1 us
  starting transfers between devices: 16.4 us -> 21.1 us
  local copies, waits for them, and re-layouts: 22.5 us -> 24.3 us
    all_gather x1 -> x0, waiting for transfers between devices: 56.9 us -> none  [body(): piece = lax.all_gather(own_field[None], 'sub', axis=0, tiled=True)]
    all_to_all x0 -> x1, waiting for transfers between devices: none -> 32.5 us  [body(): lax.all_to_all(jnp.stack([own_field[None]] * lax.axis_size('sub')), 'sub'...]
    all_to_all x0 -> x1, starting transfers between devices: none -> 4.94 us  [body(): lax.all_to_all(jnp.stack([own_field[None]] * lax.axis_size('sub')), 'sub'...]
    another operation x1 -> x2, local copies, waits for them, and re-layouts: 0.74 us -> 2.52 us  [the longest x1 1.79 us: body(): jnp.stack([own_field[None]] * lax.axis_size('sub'))]
    unnamed x16 -> x18, local copies, waits for them, and re-layouts: 17 us -> 17 us
  transfers between devices with their start and end apart: 3 -> 3, of which waited for: 3 -> 3; matrix products, arithmetic and copies ran while one was open for 13% -> 17% of each run, Pallas kernels for 0% -> 0%
where the time goes in v1:
time: 113 us; the launch traced here: 112 us
  waiting for transfers between devices  47.9 us (42%)
  local copies, waits for them, and re-layouts  24.3 us (22%)
  starting transfers between devices  21.1 us (19%)
  matrix products  12.7 us (11%)
  other arithmetic  4.63 us (4%)
    all_to_all x1, waiting for transfers between devices, body(): lax.all_to_all(jnp.stack([own_field[None]] * lax.axis_size('sub')), 'sub'...  32.5 us
    unnamed x18, local copies, waits for them, and re-layouts  17 us
    all_to_all x1, waiting for transfers between devices, body(): lax.all_to_all(picked, 'sub', split_axis=1, concat_axis=0, tiled=True)  12.7 us
    all_to_all x1, starting transfers between devices, body(): lax.all_to_all(picked, 'sub', split_axis=1, concat_axis=0, tiled=True)  10.8 us
    dot_general x1, matrix products, body(): jnp.dot(masked, ancestor_blocks.reshape(LEVELS * BW, group_cols), preferr...  6.06 us
    all_to_all x1, starting transfers between devices, body(): lax.all_to_all(regrouped, 'vec', split_axis=0, concat_axis=2, tiled=True)  5.45 us
    all_to_all x1, starting transfers between devices, body(): lax.all_to_all(jnp.stack([own_field[None]] * lax.axis_size('sub')), 'sub'...  4.94 us
    dot_general x1, matrix products, body(): jnp.einsum('lc,cbk->lbk', select, piece, preferred_element_type=jnp.float32)  3 us
  transfers between devices with their start and end apart: 3, of which 3 were waited for; matrix products, arithmetic and copies ran while one was open for 17% of the time, Pallas kernels for 0%

profile of v1, /device:TPU:8, one launch (start us, length us, event | category | flops | bytes accessed | tf_op | source)
XLA Modules:
  0.0 111.7 jit_solution(9008322832255128597)
XLA Ops:
  0.6 0.0 copy-start
  0.6 1.8 %reshape.101 = bf16[8,4,2560]{2,1,0:T(4,128)(2,1)} reshape(bf16[32,2560]{1,0:T(8,128)(2,1)} %param.7) | data formatting | bytes 327680 | tf_op jit(solution)/shard_map/reshape | solution.py:47
  2.4 5.4 %all-to-all-start = ((bf16[8,4,2560]{2,1,0:T(4,128)(2,1)}), bf16[8,4,2560]{2,1,0:T(4,128)(2,1)S(1)}, u32[]{:S(2)}, u32[]{:S(2)}) async-start(bf16[8,4,2560]{2,1,0:T(4,128)(2,1)} %reshape.101), calls=%async_computation | async-start | bytes 327680 | tf_op jit(solution)/shard_map/all_to_all | solution.py:48
  7.9 0.7 iota_compare_fusion
  8.6 0.7 copy.19
  9.4 0.1 reduce-window.9
  9.4 0.1 reduce
  9.5 0.7 and_compare_fusion.9
  10.2 2.7 %all-to-all-done = bf16[8,4,2560]{2,1,0:T(4,128)(2,1)S(1)} async-done(((bf16[8,4,2560]{2,1,0:T(4,128)(2,1)}), bf16[8,4,2560]{2,1,0:T(4,128)(2,1)S(1)}, u32[]{:S(2)}, u32[]{:S(2)}) %all-to-all-start) | async-done | bytes 163872 | tf_op jit(solution)/shard_map/all_to_all | solution.py:48
  12.9 0.8 slice_select_fusion.1
  13.8 0.1 reshape.103
  13.9 0.3 convolution_convert_fusion.1
  14.1 0.3 convolution_convert_fusion
  14.4 0.2 fusion.10
  14.6 0.2 fusion.11
  14.8 0.2 slice.64
  15.1 0.2 pad_select_fusion.7
  15.3 0.2 slice.65
  15.5 0.2 pad_select_fusion.6
  15.7 0.2 slice.66
  15.9 0.2 pad_select_fusion.5
  16.1 0.2 slice.67
  16.3 0.2 pad_select_fusion.4
  16.5 0.2 slice.68
  16.8 0.2 pad_select_fusion.3
  17.0 0.2 slice.69
  17.2 0.2 pad_select_fusion.2
  17.4 0.2 pad_select_fusion.1
  17.7 0.2 pad_select_fusion
  17.9 0.2 fusion.14
  18.1 0.9 copy.20
  19.0 10.8 %all-to-all-start.1 = ((bf16[4,32,1152]{2,0,1:T(4,128)(2,1)}), bf16[4,32,1152]{2,0,1:T(4,128)(2,1)S(1)}, u32[]{:S(2)}, u32[]{:S(2)}) async-start(bf16[4,32,1152]{2,0,1:T(4,128)(2,1)} %copy.20), calls=%async_computation.1 | async-start | bytes 589824 | tf_op jit(solution)/shard_map/all_to_all | solution.py:58
  29.7 12.7 %all-to-all-done.1 = bf16[4,32,1152]{2,0,1:T(4,128)(2,1)S(1)} async-done(((bf16[4,32,1152]{2,0,1:T(4,128)(2,1)}), bf16[4,32,1152]{2,0,1:T(4,128)(2,1)S(1)}, u32[]{:S(2)}, u32[]{:S(2)}) %all-to-all-start.1) | async-done | bytes 294944 | tf_op jit(solution)/shard_map/all_to_all | solution.py:58
  42.5 0.1 reshape.105
  42.6 0.2 convolution_convert_fusion.2
  42.7 0.0 copy-start.1
  42.8 1.8 %stack.3 = bf16[32,1,256,128]{3,2,1,0:T(8,128)(2,1)} broadcast(bf16[256,128]{1,0:T(8,128)(2,1)S(1)} %convolution_convert_fusion.2), dimensions={2,3} | broadcast | bytes 2162688 | tf_op jit(solution)/shard_map/stack | solution.py:74
  44.5 4.9 %all-to-all-start.2 = ((bf16[32,1,256,128]{3,2,1,0:T(8,128)(2,1)}), bf16[32,1,256,128]{3,2,1,0:T(8,128)(2,1)}, u32[]{:S(2)}, u32[]{:S(2)}) async-start(bf16[32,1,256,128]{3,2,1,0:T(8,128)(2,1)} %stack.3), calls=%async_computation.2 | async-start | bytes 4194304 | tf_op jit(solution)/shard_map/all_to_all | solution.py:74
  49.5 0.2 dynamic-slice_reduce_fusion
  49.7 0.5 mul.16
  50.2 6.8 %copy.29 = bf16[96,8,16,256]{3,1,2,0:T(8,128)(2,1)} copy(bf16[96,8,16,256]{3,2,1,0:T(8,128)(2,1)S(1)} %bitcast.57) | data formatting | bytes 12582912
  57.0 8.8 %copy.21 = bf16[4096,768]{0,1:T(8,128)(2,1)} copy(bf16[4096,768]{1,0:T(8,128)(2,1)} %param.12) | data formatting | bytes 12582912 | tf_op args[5]
  65.8 32.5 %all-to-all-done.2 = bf16[32,1,256,128]{3,2,1,0:T(8,128)(2,1)} async-done(((bf16[32,1,256,128]{3,2,1,0:T(8,128)(2,1)}), bf16[32,1,256,128]{3,2,1,0:T(8,128)(2,1)}, u32[]{:S(2)}, u32[]{:S(2)}) %all-to-all-start.2) | async-done | bytes 2097184 | tf_op jit(solution)/shard_map/all_to_all | solution.py:74
  98.3 3.0 %fusion.7 = bf16[3,256,128]{2,0,1:T(4,128)(2,1)S(1)} fusion(bf16[32,1,256,128]{3,2,1,0:T(8,128)(2,1)} %all-to-all-done.2, s32[3]{0:T(128)S(1)} %dynamic-slice_reduce_fusion), kind=kOutput, calls=%fused_computation.10 | convolution fusion | flops 6389856 | bytes 2293772 | tf_op jit(solution)/shard_map/lc,cbk->lbk/dot_general | solution.py:78
  101.4 0.0 slice-start.1
  101.4 6.1 %fusion = f32[4096,128]{0,1:T(8,128)S(1)} fusion(bf16[768,128]{1,0:T(8,128)(2,1)S(1)} %bitcast.61, bf16[4096,768]{0,1:T(8,128)(2,1)} %copy.21, bf16[4096,768]{0,1:T(8,128)(2,1)} %bitcast.56), kind=kOutput, calls=%fused_computation | convolution fusion | flops 808452096 | bytes 14876672 | tf_op jit(solution)/shard_map/dot_general | solution.py:86
  107.5 2.9 %fusion.3 = bf16[4096,128]{0,1:T(8,128)(2,1)S(1)} fusion(f32[4096,128]{0,1:T(8,128)S(1)} %fusion, bf16[4096,1024]{1,0:T(8,128)(2,1)S(1)} %bitcast.59, bf16[128,1152]{1,0:T(8,128)(2,1)S(1)} %reshape.105), kind=kOutput, calls=%fused_computation.4 | convolution fusion | flops 1074790400 | bytes 11796480 | tf_op jit(solution)/shard_map/dot_general | solution.py:69
  110.4 1.3 %copy.25 = bf16[4096,128]{1,0:T(8,128)(2,1)} copy(bf16[4096,128]{0,1:T(8,128)(2,1)S(1)} %fusion.3) | data formatting | bytes 2097152
  (21 shorter events, 0.2 us)
Async XLA Ops:
  0.6 41.9 %copy-start = (bf16[8192,128]{1,0:T(8,128)(2,1)S(1)}, bf16[8192,128]{1,0:T(8,128)(2,1)}, u32[]{:S(2)}) copy-start(bf16[8192,128]{1,0:T(8,128)(2,1)} %param.11) | copy-start | bytes 6291460
  2.4 10.5 %all-to-all-start = ((bf16[8,4,2560]{2,1,0:T(4,128)(2,1)}), bf16[8,4,2560]{2,1,0:T(4,128)(2,1)S(1)}, u32[]{:S(2)}, u32[]{:S(2)}) async-start(bf16[8,4,2560]{2,1,0:T(4,128)(2,1)} %reshape.101), calls=%async_computation | async-start | bytes 327680 | tf_op jit(solution)/shard_map/all_to_all | solution.py:48
  17.7 31.8 %copy-start.2 = (s32[32,3]{0,1:T(4,128)S(1)}, s32[32,3]{0,1:T(4,128)}, u32[]{:S(2)}) copy-start(s32[32,3]{0,1:T(4,128)} %param.9) | copy-start | bytes 1156
  17.7 32.0 %copy-start.3 = (s32[1,16,3]{1,0,2:T(1,128)S(1)}, s32[1,16,3]{1,0,2:T(1,128)}, u32[]{:S(2)}) copy-start(s32[1,16,3]{1,0,2:T(1,128)} %param.13) | copy-start | bytes 580
  19.0 23.5 %all-to-all-start.1 = ((bf16[4,32,1152]{2,0,1:T(4,128)(2,1)}), bf16[4,32,1152]{2,0,1:T(4,128)(2,1)S(1)}, u32[]{:S(2)}, u32[]{:S(2)}) async-start(bf16[4,32,1152]{2,0,1:T(4,128)(2,1)} %copy.20), calls=%async_computation.1 | async-start | bytes 589824 | tf_op jit(solution)/shard_map/all_to_all | solution.py:58
  42.7 7.5 %copy-start.1 = (bf16[256,128]{1,0:T(8,128)(2,1)}, bf16[256,128]{1,0:T(8,128)(2,1)S(1)}, u32[]{:S(2)}) copy-start(bf16[256,128]{1,0:T(8,128)(2,1)S(1)} %convolution_convert_fusion.2) | copy-start | bytes 196612
  44.5 53.8 %all-to-all-start.2 = ((bf16[32,1,256,128]{3,2,1,0:T(8,128)(2,1)}), bf16[32,1,256,128]{3,2,1,0:T(8,128)(2,1)}, u32[]{:S(2)}, u32[]{:S(2)}) async-start(bf16[32,1,256,128]{3,2,1,0:T(8,128)(2,1)} %stack.3), calls=%async_computation.2 | async-start | bytes 4194304 | tf_op jit(solution)/shard_map/all_to_all | solution.py:74
  98.3 9.1 %slice-start = ((s8[8388608]{0:T(1024)(128)(4,1)}), s8[4194304]{0:T(1024)(128)(4,1)S(1)}, s32[]{:S(2)}) async-start(s8[8388608]{0:T(1024)(128)(4,1)} %bitcast.58), calls=%async_computation.3 | async-start | bytes 8388608
  101.4 6.1 %slice-start.1 = ((s8[8388608]{0:T(1024)(128)(4,1)}), s8[4194304]{0:T(1024)(128)(4,1)S(1)}, s32[]{:S(2)}) async-start(s8[8388608]{0:T(1024)(128)(4,1)} %bitcast.58), calls=%async_computation.4 | async-start | bytes 8388608
